TPU v7x, 256 devices: a whole 4x4x8 slice. The times are simulated.
256 devices in a mesh: docs: 64 (over z, y, core), rep: 4 (over x).
Axes of the slice: x: 4, y: 4, z: 8, core: 2. Of those that a mesh axis runs over, the one named last changes fastest.
Arguments:
- queries: bfloat16 [32768, 1024], P(('docs', 'rep')), may hold values from -6 to 6
- adapter: bfloat16 [1024, 1024], replicated, may hold values from -0.1875 to 0.1875
- doc_table: bfloat16 [65536, 1024], P(('docs', 'rep')), may hold values from -6 to 6
- routes: int32 [32768, 4], P(('docs', 'rep')), may hold values from 0 to 255, all different within a row; in each aligned block of 128 rows (0 to 127, 128 to 255, ...) at most 4 rows name the same one
- doc_rows: int32 [32768, 4, 16], P(('docs', 'rep')), may hold values from 0 to 255, as said below
- labels: int32 [32768, 4, 16], P(('docs', 'rep')), may hold values from 0 to 4
Outputs:
- losses: float32 [32768], P(('docs', 'rep'))
- query_grads: bfloat16 [32768, 1024], P(('docs', 'rep'))
- adapter_grad: bfloat16 [1024, 1024], P('docs')
Inputs may be any that keep to these rules, and one draw needn't show every extreme that they name: `routes`: each query names 4 different owners; among the queries of one device no owner is named more than 4 times, and in every draw some owner is named exactly 4 times by some device's queries. `doc_rows`: the 16 rows of one query at one owner are distinct.
All inputs are finite; a program needn't handle non-finite values.
Results may differ from a plain program's by a relative error of at most 0.024.
Values may be sent and summed in bfloat16 or wider, within the bound.
No kernel may reach another device: no remote copies, remote signals or barrier semaphores. Data moves between devices by JAX's collectives and lax.ppermute only.
A program may use at most 128 MiB of HBM per device.

v0:
```python
import math
import jax
import jax.numpy as jnp
from jax import lax
from jax.sharding import PartitionSpec as P

EPSILON = 1e-06
LOSS_SCALE = 128.0


def unit_rows(rows):
    widened = rows.astype(jnp.float32)
    return (
        widened / jnp.sqrt(jnp.mean(widened * widened, axis=-1, keepdims=True) + EPSILON)
    ).astype(jnp.bfloat16)


def on_device(queries, adapter, doc_table, routes, doc_rows, labels):
    doc_groups = lax.axis_size("docs")
    rep_groups = lax.axis_size("rep")
    devices = doc_groups * rep_groups
    query_rows, feature_width = queries.shape
    fanout = routes.shape[1]
    per_owner = doc_rows.shape[2]
    doc_count = doc_table.shape[0]
    capacity = max(2, 2 * query_rows * fanout // devices)
    slots_all = devices * capacity
    score_scale = 2.0 / math.sqrt(feature_width)
    adapted = jnp.dot(queries, adapter, preferred_element_type=jnp.float32)
    radius = jnp.sqrt(jnp.mean(adapted * adapted, axis=-1, keepdims=True) + EPSILON)
    unit_exact = adapted / radius
    unit_query = unit_exact.astype(jnp.bfloat16)
    owner_hits = (routes[:, :, None] == jnp.arange(devices, dtype=jnp.int32)[None, None, :]).astype(
        jnp.int32
    )
    per_query = jnp.sum(owner_hits, axis=1)
    row_index = jnp.arange(query_rows, dtype=jnp.int32)
    lower_table = (row_index[:, None] > row_index[None, :]).astype(jnp.float32)
    earlier = jnp.dot(
        lower_table, per_query.astype(jnp.float32), precision=lax.Precision.HIGHEST
    ).astype(jnp.int32)
    slot_index = jnp.sum(earlier[:, None, :] * owner_hits, axis=-1)
    placed = routes * capacity + slot_index
    target_slot = placed.reshape(-1)
    repeated = jnp.broadcast_to(
        unit_query[:, None, :], (query_rows, fanout, feature_width)
    ).reshape(-1, feature_width)
    outgoing = jnp.zeros((slots_all, feature_width), jnp.bfloat16).at[target_slot].set(repeated)
    outgoing_ids = (
        jnp.zeros((slots_all, per_owner), jnp.int32)
        .at[target_slot]
        .set(doc_rows.reshape(-1, per_owner))
    )
    outgoing = outgoing.reshape(doc_groups, rep_groups, capacity, feature_width)
    outgoing_ids = outgoing_ids.reshape(doc_groups, rep_groups, capacity, per_owner)
    arrived, arrived_ids = (
        lax.all_to_all(
            lax.all_to_all(outgoing, "docs", split_axis=0, concat_axis=0, tiled=True),
            "rep",
            split_axis=1,
            concat_axis=1,
            tiled=True,
        ),
        lax.all_to_all(
            lax.all_to_all(outgoing_ids, "docs", split_axis=0, concat_axis=0, tiled=True),
            "rep",
            split_axis=1,
            concat_axis=1,
            tiled=True,
        ),
    )
    arrived = arrived.reshape(slots_all, feature_width)
    arrived_ids = arrived_ids.reshape(slots_all, per_owner)
    doc_unit = unit_rows(doc_table)
    block_scores = lax.dot_general(
        arrived, doc_unit, (((1,), (1,)), ((), ())), preferred_element_type=jnp.float32
    )
    scores_out = jnp.take_along_axis(block_scores, arrived_ids, axis=1) * score_scale
    returned = lax.all_to_all(
        lax.all_to_all(
            scores_out.reshape(doc_groups, rep_groups, capacity, per_owner).astype(jnp.bfloat16),
            "docs",
            split_axis=0,
            concat_axis=0,
            tiled=True,
        ),
        "rep",
        split_axis=1,
        concat_axis=1,
        tiled=True,
    ).astype(jnp.float32)
    scores = returned.reshape(slots_all, per_owner)[placed]
    raised = jnp.exp(scores)
    norm_total = jnp.sum(raised, axis=(1, 2))
    label_weight = jnp.exp(labels.astype(jnp.float32))
    target = label_weight / jnp.sum(label_weight, axis=(1, 2), keepdims=True)
    losses = jnp.log(norm_total) - jnp.sum(target * scores, axis=(1, 2))
    weights = (LOSS_SCALE * (raised / norm_total[:, None, None] - target)).astype(jnp.bfloat16)
    weight_slots = (
        jnp.zeros((slots_all, per_owner), jnp.bfloat16)
        .at[target_slot]
        .set(weights.reshape(-1, per_owner))
    )
    weights_in = lax.all_to_all(
        lax.all_to_all(
            weight_slots.reshape(doc_groups, rep_groups, capacity, per_owner),
            "docs",
            split_axis=0,
            concat_axis=0,
            tiled=True,
        ),
        "rep",
        split_axis=1,
        concat_axis=1,
        tiled=True,
    )
    weights_in = weights_in.reshape(slots_all, per_owner)
    spread = (
        jnp.zeros((slots_all, doc_count), jnp.bfloat16)
        .at[jnp.arange(slots_all)[:, None], arrived_ids]
        .set(weights_in)
    )
    pull_out = (jnp.dot(spread, doc_unit, preferred_element_type=jnp.float32) * score_scale).astype(
        jnp.bfloat16
    )
    pull_out = pull_out.reshape(doc_groups, rep_groups, capacity, feature_width)
    pull_back = lax.all_to_all(
        lax.all_to_all(pull_out, "docs", split_axis=0, concat_axis=0, tiled=True),
        "rep",
        split_axis=1,
        concat_axis=1,
        tiled=True,
    )
    pull_rows = pull_back.reshape(slots_all, feature_width)[placed]
    pull_total = jnp.sum(pull_rows.astype(jnp.float32), axis=1)
    projection = jnp.mean(unit_exact * pull_total, axis=-1, keepdims=True)
    adapted_grad = ((pull_total - unit_exact * projection) / radius).astype(jnp.bfloat16)
    query_grads = lax.dot_general(
        adapted_grad, adapter, (((1,), (1,)), ((), ())), preferred_element_type=jnp.float32
    ).astype(jnp.bfloat16)
    inverse_root = 1.0 / math.sqrt(query_rows * devices)
    local_terms = lax.dot_general(
        queries, adapted_grad, (((0,), (0,)), ((), ())), preferred_element_type=jnp.float32
    )
    group_terms = lax.psum(local_terms.astype(jnp.bfloat16), "rep").astype(jnp.float32)
    summed = lax.psum_scatter(group_terms, "docs", scatter_dimension=0, tiled=True)
    adapter_grad = (summed * inverse_root).astype(jnp.bfloat16)
    return (losses, query_grads, adapter_grad)


def solution(mesh):
    placed = (
        P(("docs", "rep"), None),
        P(),
        P(("docs", "rep"), None),
        P(("docs", "rep"), None),
        P(("docs", "rep"), None, None),
        P(("docs", "rep"), None, None),
    )
    return jax.shard_map(
        on_device,
        mesh=mesh,
        in_specs=placed,
        out_specs=(P(("docs", "rep")), P(("docs", "rep"), None), P("docs", None)),
        check_vma=False,
    )
```

profile of v0, /device:TPU:2, one launch (start us, length us, event | category | flops | bytes accessed | tf_op | source)
XLA Modules:
  0.0 777.8 jit_solution(13826968901884588031)
XLA Ops:
  14.1 12.1 %all-to-all-start = ((s32[64,1,256]{2,1,0:T(1,128)}), s32[64,1,256]{2,1,0:T(1,128)S(1)}, u32[]{:S(2)}, u32[]{:S(2)}) async-start(s32[64,1,256]{2,1,0:T(1,128)} %reshape.230), calls=%async_computation | async-start | bytes 131072 | tf_op jit(solution)/shard_map/all_to_all | solution.py:65
  29.1 4.8 scatter_custom_fusion.1
  33.9 4.1 reshape.145
  38.0 10.6 %all-to-all-start.2 = ((bf16[64,4,4,1024]{3,2,1,0:T(4,128)(2,1)}), bf16[64,4,4,1024]{3,2,1,0:T(4,128)(2,1)}, u32[]{:S(2)}, u32[]{:S(2)}) async-start(bf16[64,4,4,1024]{3,2,1,0:T(4,128)(2,1)} %reshape.145), calls=%async_computation.2 | async-start | bytes 4194304 | tf_op jit(solution)/shard_map/all_to_all | solution.py:58
  51.4 48.4 %all-to-all-done.2 = bf16[64,4,4,1024]{3,2,1,0:T(4,128)(2,1)} async-done(((bf16[64,4,4,1024]{3,2,1,0:T(4,128)(2,1)}), bf16[64,4,4,1024]{3,2,1,0:T(4,128)(2,1)}, u32[]{:S(2)}, u32[]{:S(2)}) %all-to-all-start.2) | async-done | bytes 2097184 | tf_op jit(solution)/shard_map/all_to_all | solution.py:58
  99.8 4.8 all-to-all-start.1
  104.6 3.7 copy.139
  108.8 5.9 all-to-all-start.3
  119.0 18.1 %all-to-all-done.3 = bf16[64,4,4,1024]{3,2,0,1:T(4,128)(2,1)} async-done(((bf16[64,4,4,1024]{3,2,0,1:T(4,128)(2,1)}), bf16[64,4,4,1024]{3,2,0,1:T(4,128)(2,1)}, u32[]{:S(2)}, u32[]{:S(2)}) %all-to-all-start.3) | async-done | bytes 2097184 | tf_op jit(solution)/shard_map/all_to_all | solution.py:57
  137.1 4.1 copy.140
  141.2 4.0 reshape.146
  147.7 129.5 %gather_fusion.2 = f32[16384]{0:T(1024)S(1)} fusion(f32[1024,256]{1,0:T(8,128)S(1)} %fusion.15, s32[16384]{0:T(1024)S(1)} %reshape.177), kind=kCustom, calls=%fused_computation.2 | custom fusion | bytes 262144 | tf_op jit(solution)/shard_map/jit(take_along_axis)/gather | solution.py:78
  279.0 6.8 all-to-all-start.4
  286.0 9.4 %all-to-all-done.4 = bf16[64,2,128]{2,1,0:T(2,128)(2,1)S(1)} async-done(((bf16[64,2,128]{2,1,0:T(2,128)(2,1)}), bf16[64,2,128]{2,1,0:T(2,128)(2,1)S(1)}, u32[]{:S(2)}, u32[]{:S(2)}) %all-to-all-start.4) | async-done | bytes 32800 | tf_op jit(solution)/shard_map/all_to_all | solution.py:80
  296.6 4.7 all-to-all-start.5
  301.4 3.9 all-to-all-done.5
  309.8 4.6 all-to-all-start.6
  314.5 9.4 %all-to-all-done.6 = bf16[64,2,128]{2,1,0:T(2,128)(2,1)S(1)} async-done(((bf16[64,2,128]{2,1,0:T(2,128)(2,1)}), bf16[64,2,128]{2,1,0:T(2,128)(2,1)S(1)}, u32[]{:S(2)}, u32[]{:S(2)}) %all-to-all-start.6) | async-done | bytes 32800 | tf_op jit(solution)/shard_map/all_to_all | solution.py:105
  325.2 4.7 all-to-all-start.7
  330.3 3.6 all-to-all-done.7
  334.4 112.7 %scatter_custom_fusion.3 = bf16[262144]{0:T(1024)(128)(2,1)S(1)} fusion(s32[16384]{0:T(1024)S(1)} %reshape.207, bf16[16384]{0:T(1024)(128)(2,1)S(1)} %reshape.209, bf16[]{:T(256)} %constant.18.clone.1), kind=kCustom, calls=%fused_computation.27 | custom fusion | bytes 524290
  448.1 3.2 multiply_convert_fusion
  451.3 4.1 reshape.153
  455.4 56.1 %all_to_all.50 = bf16[64,4,4,1024]{3,2,1,0:T(4,128)(2,1)S(1)} all-to-all(bf16[64,4,4,1024]{3,2,1,0:T(4,128)(2,1)} %reshape.153), channel_id=1, replica_groups=mesh['docs'=64,'rep'=4] {'docs'}, dimensions={0} | all-to-all | bytes 4194304 | tf_op jit(solution)/shard_map/all_to_all | solution.py:128
  512.3 27.9 %all_to_all.51 = bf16[64,4,4,1024]{3,2,0,1:T(4,128)(2,1)S(1)} all-to-all(bf16[64,4,4,1024]{3,2,0,1:T(4,128)(2,1)S(1)} %copy.155), channel_id=1, replica_groups=mesh['docs'=64,'rep'=4] {'rep'}, dimensions={1} | all-to-all | bytes 4194304 | tf_op jit(solution)/shard_map/all_to_all | solution.py:127
  542.7 4.0 reshape.154
  546.7 5.3 gather_fusion.1
  552.0 2.7 reshape.219
  554.8 2.9 reduce_sum.88
  560.2 59.0 %all-reduce.2.cloned.1.call-done = bf16[1024,1024]{0,1:T(8,128)(2,1)} async-done(((bf16[1024,1024]{0,1:T(8,128)(2,1)}), bf16[1024,1024]{0,1:T(8,128)(2,1)}) %all-reduce.2.cloned.1.call-update) | async-done | bytes 2097168 | tf_op jit(solution)/shard_map/psum | solution.py:145
  619.3 4.1 copy.158
  625.5 143.6 %reduce-scatter.4.cloned.1.call-done = f32[16,1024]{1,0:T(8,128)} async-done(((f32[1024,1024]{1,0:T(8,128)}), f32[16,1024]{1,0:T(8,128)}) %reduce-scatter.4.cloned.1.call-update) | async-done | bytes 65552
  (121 shorter events, 40.5 us)
Async XLA Ops:
  7.2 19.0 %copy-start = (bf16[1024,1024]{1,0:T(8,128)(2,1)S(1)}, bf16[1024,1024]{1,0:T(8,128)(2,1)}, u32[]{:S(2)}) copy-start(bf16[1024,1024]{1,0:T(8,128)(2,1)} %param.7) | copy-start | bytes 6291460
  7.2 19.0 %copy-start.10 = (bf16[128,1024]{1,0:T(8,128)(2,1)S(1)}, bf16[128,1024]{1,0:T(8,128)(2,1)}, u32[]{:S(2)}) copy-start(bf16[128,1024]{1,0:T(8,128)(2,1)} %param.6) | copy-start | bytes 786436
  10.3 18.8 %copy-start.16 = (s32[512,1]{0,1:T(1,128)}, s32[512,1]{0,1:T(1,128)S(1)}, u32[]{:S(2)}) copy-start(s32[512,1]{0,1:T(1,128)S(1)} %compare_select_fusion.2) | copy-start | bytes 6148
  14.1 24.0 %all-to-all-start = ((s32[64,1,256]{2,1,0:T(1,128)}), s32[64,1,256]{2,1,0:T(1,128)S(1)}, u32[]{:S(2)}, u32[]{:S(2)}) async-start(s32[64,1,256]{2,1,0:T(1,128)} %reshape.230), calls=%async_computation | async-start | bytes 131072 | tf_op jit(solution)/shard_map/all_to_all | solution.py:65
  26.7 0.8 copy-start.1
  26.8 0.8 copy-start.14
  38.0 61.7 %all-to-all-start.2 = ((bf16[64,4,4,1024]{3,2,1,0:T(4,128)(2,1)}), bf16[64,4,4,1024]{3,2,1,0:T(4,128)(2,1)}, u32[]{:S(2)}, u32[]{:S(2)}) async-start(bf16[64,4,4,1024]{3,2,1,0:T(4,128)(2,1)} %reshape.145), calls=%async_computation.2 | async-start | bytes 4194304 | tf_op jit(solution)/shard_map/all_to_all | solution.py:58
  99.8 9.0 %all-to-all-start.1 = ((s32[4,1,4096]{2,1,0:T(1,128)}), s32[4,1,4096]{2,1,0:T(1,128)S(1)}, u32[]{:S(2)}, u32[]{:S(2)}) async-start(s32[4,1,4096]{2,1,0:T(1,128)} %reshape.232), calls=%async_computation.1 | async-start | bytes 131072 | tf_op jit(solution)/shard_map/all_to_all | solution.py:64
  108.3 7.1 copy-start.8
  108.3 7.7 copy-start.6
  108.8 28.3 %all-to-all-start.3 = ((bf16[64,4,4,1024]{3,2,0,1:T(4,128)(2,1)}), bf16[64,4,4,1024]{3,2,0,1:T(4,128)(2,1)}, u32[]{:S(2)}, u32[]{:S(2)}) async-start(bf16[64,4,4,1024]{3,2,0,1:T(4,128)(2,1)} %copy.139), calls=%async_computation.3 | async-start | bytes 4194304 | tf_op jit(solution)/shard_map/all_to_all | solution.py:57
  116.2 28.9 %copy-start.17 = (f32[256]{0:T(256)}, f32[256]{0:T(256)S(1)}, u32[]{:S(2)}) copy-start(f32[256]{0:T(256)S(1)} %add_sqrt_fusion) | copy-start | bytes 3076
  117.2 0.7 copy-start.4
  147.7 130.2 %copy-start.5 = (s32[4,4,16,64]{3,2,1,0:T(8,128)S(1)}, s32[4,4,16,64]{3,2,1,0:T(8,128)}, u32[]{:S(2)}) copy-start(s32[4,4,16,64]{3,2,1,0:T(8,128)} %copy-done.4) | copy-start | bytes 196612
  277.2 8.6 %copy-start.12 = (s32[512]{0:T(512)S(1)}, s32[512]{0:T(512)}, u32[]{:S(2)}) copy-start(s32[512]{0:T(512)} %reshape.163) | copy-start | bytes 6148
  277.2 8.6 %copy-start.3 = (s32[1024,16,1]{1,0,2:T(8,128)S(1)}, s32[1024,16,1]{1,0,2:T(8,128)}, u32[]{:S(2)}) copy-start(s32[1024,16,1]{1,0,2:T(8,128)} %get-tuple-element.31) | copy-start | bytes 196612
  277.2 24.1 %copy-start.20 = (s32[2]{0:T(128)S(1)}, s32[2]{0:T(128)}, u32[]{:S(2)}) copy-start(s32[2]{0:T(128)} %constant.59) | copy-start | bytes 28
  279.0 16.3 %all-to-all-start.4 = ((bf16[64,2,128]{2,1,0:T(2,128)(2,1)}), bf16[64,2,128]{2,1,0:T(2,128)(2,1)S(1)}, u32[]{:S(2)}, u32[]{:S(2)}) async-start(bf16[64,2,128]{2,1,0:T(2,128)(2,1)} %reshape.234), calls=%async_computation.4 | async-start | bytes 65536 | tf_op jit(solution)/shard_map/all_to_all | solution.py:80
  295.5 11.3 %copy-start.9 = (s32[128,4,16]{0,2,1:T(8,128)S(1)}, s32[128,4,16]{0,2,1:T(8,128)}, u32[]{:S(2)}) copy-start(s32[128,4,16]{0,2,1:T(8,128)} %param.11) | copy-start | bytes 98308
  295.5 11.3 %copy-start.13 = (f32[128]{0:T(128)S(1)}, f32[128]{0:T(128)}, u32[]{:S(2)}) copy-start(f32[128]{0:T(128)} %fusion.12) | copy-start | bytes 1540
  296.6 8.7 %all-to-all-start.5 = ((bf16[4,2,2048]{2,1,0:T(2,128)(2,1)}), bf16[4,2,2048]{2,1,0:T(2,128)(2,1)S(1)}, u32[]{:S(2)}, u32[]{:S(2)}) async-start(bf16[4,2,2048]{2,1,0:T(2,128)(2,1)} %reshape.236), calls=%async_computation.5 | async-start | bytes 65536 | tf_op jit(solution)/shard_map/all_to_all | solution.py:79
  305.4 9.1 %copy-start.19 = (s32[2]{0:T(128)S(1)}, s32[2]{0:T(128)}, u32[]{:S(2)}) copy-start(s32[2]{0:T(128)} %constant.56) | copy-start | bytes 28
  309.8 14.1 %all-to-all-start.6 = ((bf16[64,2,128]{2,1,0:T(2,128)(2,1)}), bf16[64,2,128]{2,1,0:T(2,128)(2,1)S(1)}, u32[]{:S(2)}, u32[]{:S(2)}) async-start(bf16[64,2,128]{2,1,0:T(2,128)(2,1)} %reshape.238), calls=%async_computation.6 | async-start | bytes 65536 | tf_op jit(solution)/shard_map/all_to_all | solution.py:105
  324.2 123.9 %copy-start.7 = (bf16[256,1024]{1,0:T(8,128)(2,1)S(1)}, bf16[256,1024]{1,0:T(8,128)(2,1)}, u32[]{:S(2)}) copy-start(bf16[256,1024]{1,0:T(8,128)(2,1)} %param.8) | copy-start | bytes 1572868
  324.2 123.9 %copy-start.18 = (f32[256]{0:T(256)S(1)}, f32[256]{0:T(256)}, u32[]{:S(2)}) copy-start(f32[256]{0:T(256)} %copy-done.17) | copy-start | bytes 3076
  325.2 8.7 %all-to-all-start.7 = ((bf16[4,2,2048]{2,1,0:T(2,128)(2,1)}), bf16[4,2,2048]{2,1,0:T(2,128)(2,1)S(1)}, u32[]{:S(2)}, u32[]{:S(2)}) async-start(bf16[4,2,2048]{2,1,0:T(2,128)(2,1)} %reshape.240), calls=%async_computation.7 | async-start | bytes 65536 | tf_op jit(solution)/shard_map/all_to_all | solution.py:104
  329.9 289.4 %all-reduce.2.cloned.1.call-start = ((), (), s32[]{:S(2)}) async-start(), calls=%async_computation.11 | async-start | bytes 4194304 | tf_op jit(solution)/shard_map/psum | solution.py:145
  554.8 2.9 copy-start.2
  554.8 2.9 copy-start.15
  554.8 3.2 copy-start.11
  560.2 208.9 %reduce-scatter.4.cloned.1.call-start = ((), (), s32[]{:S(2)}) async-start(), calls=%async_computation.12 | async-start | bytes 4259840
Sparse Core Ops, SparseCore 0:
  560.3 58.9 all-reduce.1
  623.5 145.5 reduce-scatter.3
where the time goes:
time: 779 us; the launch traced here: 778 us
  local copies, waits for them, and re-layouts  309 us (40%)
  waiting for transfers between devices  296 us (38%)
  blocking collectives  83.9 us (11%)
  starting transfers between devices  54.1 us (7%)
  between operations  14.5 us (2%)
  matrix products  10.2 us (1%)
  other arithmetic  10.1 us (1%)
    unnamed x3, waiting for transfers between devices  144 us
    gather x5, local copies, waits for them, and re-layouts, on_device(): jnp.take_along_axis(block_scores, arrived_ids, axis=1) * score_scale  130 us
    unnamed x61, local copies, waits for them, and re-layouts  127 us
    psum x1, waiting for transfers between devices, on_device(): lax.psum(local_terms.astype(jnp.bfloat16), 'rep').astype(jnp.float32)  59 us
    all_to_all x1, blocking collectives, on_device(): lax.all_to_all(pull_out, 'docs', split_axis=0, concat_axis=0, tiled=True)  56.1 us
    all_to_all x1, waiting for transfers between devices, on_device(): lax.all_to_all(outgoing, 'docs', split_axis=0, concat_axis=0, tiled=True)  48.4 us
    all_to_all x1, blocking collectives, on_device(): lax.all_to_all(lax.all_to_all(pull_out, 'docs', split_axis=0, concat_axis...  27.9 us
    all_to_all x1, waiting for transfers between devices, on_device(): lax.all_to_all(lax.all_to_all(outgoing, 'docs', split_axis=0, concat_axis...  18.1 us
  transfers between devices with their start and end apart: 10, of which 9 were waited for; matrix products, arithmetic and copies ran while one was open for 3% of the time, Pallas kernels for 0%

commit v1 on v0

--- a/solution.py
+++ b/solution.py
@@ -142,7 +142,11 @@
     local_terms = lax.dot_general(
         queries, adapted_grad, (((0,), (0,)), ((), ())), preferred_element_type=jnp.float32
     )
-    group_terms = lax.psum(local_terms.astype(jnp.bfloat16), "rep").astype(jnp.float32)
+
+    def clear_halves(buf):
+        return jnp.sum(jax.lax.all_gather(buf, "rep"), axis=0)
+
+    group_terms = clear_halves(local_terms.astype(jnp.bfloat16)).astype(jnp.float32)
     summed = lax.psum_scatter(group_terms, "docs", scatter_dimension=0, tiled=True)
     adapter_grad = (summed * inverse_root).astype(jnp.bfloat16)
     return (losses, query_grads, adapter_grad)

time: 779 us -> 839 us (1.077); the launches traced: 778 us -> 829 us
  waiting for transfers between devices: 296 us -> 319 us
  local copies, waits for them, and re-layouts: 309 us -> 323 us
  other arithmetic: 10.1 us -> 23 us
    all_gather x0 -> x1, waiting for transfers between devices: none -> 82.1 us  [clear_halves(): return jnp.sum(jax.lax.all_gather(buf, 'rep'), axis=0)]
    psum x1 -> x0, waiting for transfers between devices: 59 us -> none  [on_device(): lax.psum(local_terms.astype(jnp.bfloat16), 'rep').astype(jnp.float32)]
    all_gather x0 -> x1, local copies, waits for them, and re-layouts: none -> 14.6 us  [clear_halves(): return jnp.sum(jax.lax.all_gather(buf, 'rep'), axis=0)]
    reduce_sum x0 -> x1, other arithmetic: none -> 12.9 us  [clear_halves(): return jnp.sum(jax.lax.all_gather(buf, 'rep'), axis=0)]
where the time goes in v1:
time: 839 us; the launch traced here: 829 us
  local copies, waits for them, and re-layouts  323 us (38%)
  waiting for transfers between devices  319 us (38%)
  blocking collectives  84.1 us (10%)
  starting transfers between devices  54.8 us (7%)
  other arithmetic  23 us (3%)
  between operations  14.8 us (2%)
  matrix products  10.2 us (1%)
    unnamed x3, waiting for transfers between devices  144 us
    gather x5, local copies, waits for them, and re-layouts, on_device(): jnp.take_along_axis(block_scores, arrived_ids, axis=1) * score_scale  130 us
    unnamed x61, local copies, waits for them, and re-layouts  127 us
    all_gather x1, waiting for transfers between devices, clear_halves(): return jnp.sum(jax.lax.all_gather(buf, 'rep'), axis=0)  82.1 us
    all_to_all x1, blocking collectives, on_device(): lax.all_to_all(pull_out, 'docs', split_axis=0, concat_axis=0, tiled=True)  56.1 us
    all_to_all x1, waiting for transfers between devices, on_device(): lax.all_to_all(outgoing, 'docs', split_axis=0, concat_axis=0, tiled=True)  48.4 us
    all_to_all x1, blocking collectives, on_device(): lax.all_to_all(lax.all_to_all(pull_out, 'docs', split_axis=0, concat_axis...  28.1 us
    all_to_all x1, waiting for transfers between devices, on_device(): lax.all_to_all(lax.all_to_all(outgoing, 'docs', split_axis=0, concat_axis...  18.1 us
  transfers between devices with their start and end apart: 10, of which 9 were waited for; matrix products, arithmetic and copies ran while one was open for 3% of the time, Pallas kernels for 0%

profile of v1, /device:TPU:2, one launch (start us, length us, event | category | flops | bytes accessed | tf_op | source)
XLA Modules:
  0.0 829.1 jit_solution(5042912573866345504)
XLA Ops:
  14.1 12.1 %all-to-all-start = ((s32[64,1,256]{2,1,0:T(1,128)}), s32[64,1,256]{2,1,0:T(1,128)S(1)}, u32[]{:S(2)}, u32[]{:S(2)}) async-start(s32[64,1,256]{2,1,0:T(1,128)} %reshape.231), calls=%async_computation | async-start | bytes 131072 | tf_op jit(solution)/shard_map/all_to_all | solution.py:65
  29.1 4.8 scatter_custom_fusion.1
  33.9 4.1 reshape.145
  38.0 10.6 %all-to-all-start.2 = ((bf16[64,4,4,1024]{3,2,1,0:T(4,128)(2,1)}), bf16[64,4,4,1024]{3,2,1,0:T(4,128)(2,1)}, u32[]{:S(2)}, u32[]{:S(2)}) async-start(bf16[64,4,4,1024]{3,2,1,0:T(4,128)(2,1)} %reshape.145), calls=%async_computation.2 | async-start | bytes 4194304 | tf_op jit(solution)/shard_map/all_to_all | solution.py:58
  51.4 48.4 %all-to-all-done.2 = bf16[64,4,4,1024]{3,2,1,0:T(4,128)(2,1)} async-done(((bf16[64,4,4,1024]{3,2,1,0:T(4,128)(2,1)}), bf16[64,4,4,1024]{3,2,1,0:T(4,128)(2,1)}, u32[]{:S(2)}, u32[]{:S(2)}) %all-to-all-start.2) | async-done | bytes 2097184 | tf_op jit(solution)/shard_map/all_to_all | solution.py:58
  99.8 4.8 all-to-all-start.1
  104.6 3.7 copy.137
  108.8 6.3 all-to-all-start.3
  119.5 18.1 %all-to-all-done.3 = bf16[64,4,4,1024]{3,2,0,1:T(4,128)(2,1)} async-done(((bf16[64,4,4,1024]{3,2,0,1:T(4,128)(2,1)}), bf16[64,4,4,1024]{3,2,0,1:T(4,128)(2,1)}, u32[]{:S(2)}, u32[]{:S(2)}) %all-to-all-start.3) | async-done | bytes 2097184 | tf_op jit(solution)/shard_map/all_to_all | solution.py:57
  137.5 4.1 copy.138
  141.6 4.0 reshape.146
  148.1 129.5 %gather_fusion.2 = f32[16384]{0:T(1024)S(1)} fusion(f32[1024,256]{1,0:T(8,128)S(1)} %fusion.15, s32[16384]{0:T(1024)S(1)} %reshape.177), kind=kCustom, calls=%fused_computation.2 | custom fusion | bytes 262144 | tf_op jit(solution)/shard_map/jit(take_along_axis)/gather | solution.py:78
  279.5 6.8 all-to-all-start.4
  286.4 9.4 %all-to-all-done.4 = bf16[64,2,128]{2,1,0:T(2,128)(2,1)S(1)} async-done(((bf16[64,2,128]{2,1,0:T(2,128)(2,1)}), bf16[64,2,128]{2,1,0:T(2,128)(2,1)S(1)}, u32[]{:S(2)}, u32[]{:S(2)}) %all-to-all-start.4) | async-done | bytes 32800 | tf_op jit(solution)/shard_map/all_to_all | solution.py:80
  297.0 4.7 all-to-all-start.5
  301.8 3.9 all-to-all-done.5
  310.3 4.6 all-to-all-start.6
  315.0 9.4 %all-to-all-done.6 = bf16[64,2,128]{2,1,0:T(2,128)(2,1)S(1)} async-done(((bf16[64,2,128]{2,1,0:T(2,128)(2,1)}), bf16[64,2,128]{2,1,0:T(2,128)(2,1)S(1)}, u32[]{:S(2)}, u32[]{:S(2)}) %all-to-all-start.6) | async-done | bytes 32800 | tf_op jit(solution)/shard_map/all_to_all | solution.py:105
  325.6 4.7 all-to-all-start.7
  330.9 3.4 all-to-all-done.7
  334.9 112.7 %scatter_custom_fusion.3 = bf16[262144]{0:T(1024)(128)(2,1)S(1)} fusion(s32[16384]{0:T(1024)S(1)} %reshape.207, bf16[16384]{0:T(1024)(128)(2,1)S(1)} %reshape.209, bf16[]{:T(256)} %constant.18.clone.1), kind=kCustom, calls=%fused_computation.27 | custom fusion | bytes 524290
  448.6 3.2 multiply_convert_fusion
  451.8 4.1 reshape.153
  455.9 56.1 %all_to_all.50 = bf16[64,4,4,1024]{3,2,1,0:T(4,128)(2,1)S(1)} all-to-all(bf16[64,4,4,1024]{3,2,1,0:T(4,128)(2,1)} %reshape.153), channel_id=1, replica_groups=mesh['docs'=64,'rep'=4] {'docs'}, dimensions={0} | all-to-all | bytes 4194304 | tf_op jit(solution)/shard_map/all_to_all | solution.py:128
  512.8 28.1 %all_to_all.51 = bf16[64,4,4,1024]{3,2,0,1:T(4,128)(2,1)S(1)} all-to-all(bf16[64,4,4,1024]{3,2,0,1:T(4,128)(2,1)S(1)} %copy.153), channel_id=1, replica_groups=mesh['docs'=64,'rep'=4] {'rep'}, dimensions={1} | all-to-all | bytes 4194304 | tf_op jit(solution)/shard_map/all_to_all | solution.py:127
  543.4 4.0 reshape.154
  547.3 5.3 gather_fusion.1
  560.9 82.1 %all-gather.3.cloned.1.call-done = bf16[4096,1024]{0,1:T(8,128)(2,1)} async-done(((bf16[1024,1024]{0,1:T(8,128)(2,1)}), bf16[4096,1024]{0,1:T(8,128)(2,1)}) %all-gather.3.cloned.1.call-update) | async-done | bytes 8388624 | tf_op jit(solution)/shard_map/all_gather | solution.py:147
  643.0 14.6 %reshape.213 = bf16[4,1024,1024]{1,0,2:T(4,128)(2,1)} reshape(bf16[4096,1024]{0,1:T(8,128)(2,1)} %all-gather.3.cloned.1.call-done) | data formatting | bytes 16777216 | tf_op jit(solution)/shard_map/all_gather | solution.py:147
  657.5 12.9 %reduce_sum.102 = bf16[1024,1024]{0,1:T(8,128)(2,1)} reduce(bf16[4,1024,1024]{1,0,2:T(4,128)(2,1)} %reshape.213, bf16[]{:T(256)} %constant.18.clone.1), dimensions={0}, to_apply=%region_13.14 | reduce | flops 3145728 | bytes 10485762 | tf_op jit(solution)/shard_map/reduce_sum | solution.py:147
  670.4 4.1 copy.156
  676.6 143.6 %reduce-scatter.4.cloned.1.call-done = f32[16,1024]{1,0:T(8,128)} async-done(((f32[1024,1024]{1,0:T(8,128)}), f32[16,1024]{1,0:T(8,128)}) %reduce-scatter.4.cloned.1.call-update) | async-done | bytes 65552
  (123 shorter events, 46.3 us)
Async XLA Ops:
  7.2 19.0 %copy-start = (bf16[1024,1024]{1,0:T(8,128)(2,1)S(1)}, bf16[1024,1024]{1,0:T(8,128)(2,1)}, u32[]{:S(2)}) copy-start(bf16[1024,1024]{1,0:T(8,128)(2,1)} %param.7) | copy-start | bytes 6291460
  7.2 19.0 %copy-start.10 = (bf16[128,1024]{1,0:T(8,128)(2,1)S(1)}, bf16[128,1024]{1,0:T(8,128)(2,1)}, u32[]{:S(2)}) copy-start(bf16[128,1024]{1,0:T(8,128)(2,1)} %param.6) | copy-start | bytes 786436
  10.3 18.8 %copy-start.16 = (s32[512,1]{0,1:T(1,128)}, s32[512,1]{0,1:T(1,128)S(1)}, u32[]{:S(2)}) copy-start(s32[512,1]{0,1:T(1,128)S(1)} %compare_select_fusion.2) | copy-start | bytes 6148
  14.1 24.0 %all-to-all-start = ((s32[64,1,256]{2,1,0:T(1,128)}), s32[64,1,256]{2,1,0:T(1,128)S(1)}, u32[]{:S(2)}, u32[]{:S(2)}) async-start(s32[64,1,256]{2,1,0:T(1,128)} %reshape.231), calls=%async_computation | async-start | bytes 131072 | tf_op jit(solution)/shard_map/all_to_all | solution.py:65
  26.7 0.8 copy-start.1
  26.8 0.8 copy-start.14
  38.0 61.7 %all-to-all-start.2 = ((bf16[64,4,4,1024]{3,2,1,0:T(4,128)(2,1)}), bf16[64,4,4,1024]{3,2,1,0:T(4,128)(2,1)}, u32[]{:S(2)}, u32[]{:S(2)}) async-start(bf16[64,4,4,1024]{3,2,1,0:T(4,128)(2,1)} %reshape.145), calls=%async_computation.2 | async-start | bytes 4194304 | tf_op jit(solution)/shard_map/all_to_all | solution.py:58
  99.8 9.0 %all-to-all-start.1 = ((s32[4,1,4096]{2,1,0:T(1,128)}), s32[4,1,4096]{2,1,0:T(1,128)S(1)}, u32[]{:S(2)}, u32[]{:S(2)}) async-start(s32[4,1,4096]{2,1,0:T(1,128)} %reshape.233), calls=%async_computation.1 | async-start | bytes 131072 | tf_op jit(solution)/shard_map/all_to_all | solution.py:64
  108.3 7.6 copy-start.8
  108.3 8.2 copy-start.6
  108.8 28.7 %all-to-all-start.3 = ((bf16[64,4,4,1024]{3,2,0,1:T(4,128)(2,1)}), bf16[64,4,4,1024]{3,2,0,1:T(4,128)(2,1)}, u32[]{:S(2)}, u32[]{:S(2)}) async-start(bf16[64,4,4,1024]{3,2,0,1:T(4,128)(2,1)} %copy.137), calls=%async_computation.3 | async-start | bytes 4194304 | tf_op jit(solution)/shard_map/all_to_all | solution.py:57
  116.7 28.9 %copy-start.17 = (f32[256]{0:T(256)}, f32[256]{0:T(256)S(1)}, u32[]{:S(2)}) copy-start(f32[256]{0:T(256)S(1)} %add_sqrt_fusion) | copy-start | bytes 3076
  117.6 0.7 copy-start.4
  148.1 130.2 %copy-start.5 = (s32[4,4,16,64]{3,2,1,0:T(8,128)S(1)}, s32[4,4,16,64]{3,2,1,0:T(8,128)}, u32[]{:S(2)}) copy-start(s32[4,4,16,64]{3,2,1,0:T(8,128)} %copy-done.4) | copy-start | bytes 196612
  277.6 8.6 %copy-start.12 = (s32[512]{0:T(512)S(1)}, s32[512]{0:T(512)}, u32[]{:S(2)}) copy-start(s32[512]{0:T(512)} %reshape.163) | copy-start | bytes 6148
  277.6 8.6 %copy-start.3 = (s32[1024,16,1]{1,0,2:T(8,128)S(1)}, s32[1024,16,1]{1,0,2:T(8,128)}, u32[]{:S(2)}) copy-start(s32[1024,16,1]{1,0,2:T(8,128)} %get-tuple-element.25) | copy-start | bytes 196612
  277.6 24.1 %copy-start.20 = (s32[2]{0:T(128)S(1)}, s32[2]{0:T(128)}, u32[]{:S(2)}) copy-start(s32[2]{0:T(128)} %constant.60) | copy-start | bytes 28
  279.5 16.3 %all-to-all-start.4 = ((bf16[64,2,128]{2,1,0:T(2,128)(2,1)}), bf16[64,2,128]{2,1,0:T(2,128)(2,1)S(1)}, u32[]{:S(2)}, u32[]{:S(2)}) async-start(bf16[64,2,128]{2,1,0:T(2,128)(2,1)} %reshape.235), calls=%async_computation.4 | async-start | bytes 65536 | tf_op jit(solution)/shard_map/all_to_all | solution.py:80
  296.0 11.3 %copy-start.9 = (s32[128,4,16]{0,2,1:T(8,128)S(1)}, s32[128,4,16]{0,2,1:T(8,128)}, u32[]{:S(2)}) copy-start(s32[128,4,16]{0,2,1:T(8,128)} %param.11) | copy-start | bytes 98308
  296.0 11.3 %copy-start.13 = (f32[128]{0:T(128)S(1)}, f32[128]{0:T(128)}, u32[]{:S(2)}) copy-start(f32[128]{0:T(128)} %fusion.12) | copy-start | bytes 1540
  297.0 8.7 %all-to-all-start.5 = ((bf16[4,2,2048]{2,1,0:T(2,128)(2,1)}), bf16[4,2,2048]{2,1,0:T(2,128)(2,1)S(1)}, u32[]{:S(2)}, u32[]{:S(2)}) async-start(bf16[4,2,2048]{2,1,0:T(2,128)(2,1)} %reshape.237), calls=%async_computation.5 | async-start | bytes 65536 | tf_op jit(solution)/shard_map/all_to_all | solution.py:79
  305.8 9.1 %copy-start.19 = (s32[2]{0:T(128)S(1)}, s32[2]{0:T(128)}, u32[]{:S(2)}) copy-start(s32[2]{0:T(128)} %constant.57) | copy-start | bytes 28
  310.3 14.1 %all-to-all-start.6 = ((bf16[64,2,128]{2,1,0:T(2,128)(2,1)}), bf16[64,2,128]{2,1,0:T(2,128)(2,1)S(1)}, u32[]{:S(2)}, u32[]{:S(2)}) async-start(bf16[64,2,128]{2,1,0:T(2,128)(2,1)} %reshape.239), calls=%async_computation.6 | async-start | bytes 65536 | tf_op jit(solution)/shard_map/all_to_all | solution.py:105
  324.6 123.9 %copy-start.7 = (bf16[256,1024]{1,0:T(8,128)(2,1)S(1)}, bf16[256,1024]{1,0:T(8,128)(2,1)}, u32[]{:S(2)}) copy-start(bf16[256,1024]{1,0:T(8,128)(2,1)} %param.8) | copy-start | bytes 1572868
  324.6 123.9 %copy-start.18 = (f32[256]{0:T(256)S(1)}, f32[256]{0:T(256)}, u32[]{:S(2)}) copy-start(f32[256]{0:T(256)} %copy-done.17) | copy-start | bytes 3076
  325.6 8.7 %all-to-all-start.7 = ((bf16[4,2,2048]{2,1,0:T(2,128)(2,1)}), bf16[4,2,2048]{2,1,0:T(2,128)(2,1)S(1)}, u32[]{:S(2)}, u32[]{:S(2)}) async-start(bf16[4,2,2048]{2,1,0:T(2,128)(2,1)} %reshape.241), calls=%async_computation.7 | async-start | bytes 65536 | tf_op jit(solution)/shard_map/all_to_all | solution.py:104
  330.3 312.6 %all-gather.3.cloned.1.call-start = ((), (), s32[]{:S(2)}) async-start(), calls=%async_computation.11 | async-start | bytes 10485760 | tf_op jit(solution)/shard_map/all_gather | solution.py:147
  555.4 2.9 copy-start.2
  555.4 2.9 copy-start.15
  555.4 3.2 copy-start.11
  560.9 259.4 %reduce-scatter.4.cloned.1.call-start = ((), (), s32[]{:S(2)}) async-start(), calls=%async_computation.12 | async-start | bytes 4259840
Sparse Core Ops, SparseCore 0:
  561.0 81.9 all-gather.2
  674.7 145.5 reduce-scatter.3
